TPU v7x, 32 devices: a whole 2x2x4 slice. The times are simulated.
32 devices in a mesh: ctx: 4 (over y, x), dp: 8 (over z, core).
Axes of the slice: x: 2, y: 2, z: 4, core: 2. Of those that a mesh axis runs over, the one named last changes fastest.
Arguments:
- queries: bfloat16 [8, 512, 1024], P('dp', 'ctx'), may hold values from -6 to 6
- keys_in: bfloat16 [8, 512, 256], P('dp', 'ctx'), may hold values from -6 to 6
- values_in: bfloat16 [8, 512, 256], P('dp', 'ctx'), may hold values from -6 to 6
- patch_order: int32 [8, 4, 128], P('dp', 'ctx'), may hold values from 0 to 127, each once within a row
- block_mask: int32 [8, 16, 8], P('dp', 'ctx'), may hold values 0 or 1
- out_weight: bfloat16 [1024, 1024], P('dp'), may hold values from -0.1875 to 0.1875
- cotangent: bfloat16 [8, 512, 1024], P('dp', 'ctx'), may hold values from -6 to 6
Outputs:
- mixed: bfloat16 [8, 512, 1024], P('dp', 'ctx')
- grad_queries: bfloat16 [8, 512, 1024], P('dp', 'ctx')
- grad_keys: bfloat16 [8, 512, 256], P('dp', 'ctx')
- grad_values: bfloat16 [8, 512, 256], P('dp', 'ctx')
- grad_weight: float32 [1024, 1024], P('dp', 'ctx')
Inputs may be any that keep to these rules, and one draw needn't show every extreme that they name: `patch_order`: each row of 128 entries is a permutation.
All inputs are finite; a program needn't handle non-finite values. No bound on the sum of `block_mask` on one device may be relied on, other than what follows from the above.
Results may differ from a plain program's by a relative error of at most 0.015.
Values may be sent and summed in bfloat16 or wider, within the bound.
No kernel may reach another device: no remote copies, remote signals or barrier semaphores. Data moves between devices by JAX's collectives and lax.ppermute only.
A program may use at most 64 MiB of HBM per device.

v0:
```python
import functools
import math

import jax
import jax.numpy as jnp
from jax import lax
from jax.experimental import pallas as pl
from jax.experimental.pallas import tpu as pltpu
from jax.sharding import PartitionSpec as P

QUERY_HEADS = 8
KEY_VALUE_HEADS = 2
HEAD_WIDTH = 128
BLK = 32
PAIRS = QUERY_HEADS // 2
HALO_ROWS = 8


F32 = jnp.float32
BF16 = jnp.bfloat16
NN = (((1,), (0,)), ((), ()))
NT = (((1,), (1,)), ((), ()))
TN = (((0,), (0,)), ((), ()))


def dot(a, b, dims):
    return lax.dot_general(a, b, dims, preferred_element_type=F32)


def vmem():
    return pl.BlockSpec(memory_space=pltpu.VMEM)


def hbm():
    return pl.BlockSpec(memory_space=pltpu.HBM)


def in_hbm(*arrays):
    return tuple(pltpu.with_memory_space_constraint(a, pltpu.HBM) for a in arrays)


def call(body, outs, specs, args, scratch=(), flops=1 << 20, room=16 << 20):
    moved = sum(a.size * a.dtype.itemsize for a in (*args, *outs))
    return pl.pallas_call(
        body,
        out_shape=outs,
        in_specs=specs,
        out_specs=[vmem() for _ in outs],
        scratch_shapes=list(scratch),
        cost_estimate=pl.CostEstimate(flops=flops, bytes_accessed=moved, transcendentals=0),
        compiler_params=pltpu.CompilerParams(vmem_limit_bytes=room),
    )(*args)


def shape(dims, dtype=BF16):
    return jax.ShapeDtypeStruct(dims, dtype)


def pack_body(k_ref, v_ref, order_ref, out_ref, order_scr, sem):
    tokens, width = k_ref.shape
    copies = [
        pltpu.make_async_copy(order_ref, order_scr, sem.at[0]),
        pltpu.make_async_copy(k_ref, out_ref.at[:tokens, :width], sem.at[1]),
        pltpu.make_async_copy(v_ref, out_ref.at[:tokens, width:], sem.at[2]),
    ]
    for c in copies:
        c.start()
    copies[0].wait()
    row = lax.broadcasted_iota(jnp.int32, (tokens, tokens), 0)
    holds = (row == order_scr[...]).astype(F32).astype(BF16)
    block = lax.broadcasted_iota(jnp.int32, (HALO_ROWS, tokens), 1) // BLK
    out_ref[tokens:, :] = jnp.zeros((HALO_ROWS, 2 * width), BF16)
    out_ref[tokens:, :tokens] = dot(block.astype(F32).astype(BF16), holds, NT).astype(BF16)
    copies[1].wait()
    copies[2].wait()


def fetch_body(a_ref, b_ref, mask_ref, a_out, b_out, table_out, mask_scr, sem):
    copies = [
        pltpu.make_async_copy(mask_ref, mask_scr, sem.at[0]),
        pltpu.make_async_copy(a_ref, a_out, sem.at[1]),
        pltpu.make_async_copy(b_ref, b_out, sem.at[2]),
    ]
    for c in copies:
        c.start()
    copies[0].wait()
    rows, columns = mask_ref.shape
    sub = lax.broadcasted_iota(jnp.int32, (HALO_ROWS, table_out.shape[1]), 0)
    for kb in range(columns):
        spread = jnp.zeros(sub.shape, F32)
        for b in range(rows):
            spread = jnp.where(sub == b, mask_scr[b, kb].astype(F32), spread)
        table_out[kb * HALO_ROWS : (kb + 1) * HALO_ROWS, :] = spread
    copies[1].wait()
    copies[2].wait()


def seen(table_ref, first, blocks, key_block, query_block):
    sub = lax.broadcasted_iota(jnp.int32, key_block.shape, 0)
    table = jnp.zeros(key_block.shape, F32)
    for kb in range(blocks):
        at = (first + kb) * HALO_ROWS
        table = jnp.where(key_block == kb, table_ref[at : at + HALO_ROWS, :], table)
    one_hot = (sub == query_block).astype(F32)
    return dot(table.astype(BF16), one_hot.astype(BF16), TN)


def forward_body(scale, place, side, q_ref, prev_ref, own_ref, next_ref, table_ref, prob_ref, attf_ref, att_ref):
    head, _ = place()
    tokens = q_ref.shape[0]
    width = own_ref.shape[1] // 2
    blocks = table_ref.shape[0] // HALO_ROWS // 2
    ids = [r[tokens:, :tokens].astype(F32).astype(jnp.int32) for r in (prev_ref, own_ref, next_ref)]
    see_prev = seen(table_ref, 0, blocks, ids[0], ids[1]) > 0.5
    see_next = seen(table_ref, blocks, blocks, ids[2], ids[1]) > 0.5
    band = (prev_ref, own_ref, next_ref)
    for g in range(KEY_VALUE_HEADS):
        keys = band_of(band, tokens, g * HEAD_WIDTH)
        values_t = band_of(band, tokens, width + g * HEAD_WIDTH).T
        for pair in range(g * PAIRS // KEY_VALUE_HEADS, (g + 1) * PAIRS // KEY_VALUE_HEADS):
            at = head_at(pair)
            scores = dot(keys, q_ref[:, head_at(2 * pair + lax.rem(head(side), 2))], NT) * scale
            low = jnp.where(see_prev, scores[:tokens], -1e30)
            mid = scores[tokens : 2 * tokens]
            high = jnp.where(see_next, scores[2 * tokens :], -1e30)
            top = jnp.maximum(jnp.maximum(low, mid), high).max(axis=0, keepdims=True)
            low, mid, high = jnp.exp(low - top), jnp.exp(mid - top), jnp.exp(high - top)
            inverse = 1.0 / (low + mid + high).sum(axis=0, keepdims=True)
            prob = jnp.concatenate([low * inverse, mid * inverse, high * inverse], 0).astype(BF16)
            prob_ref[:, at] = prob
            att = dot(values_t, prob, NN)
            attf_ref[at, :] = att
            att_ref[at, :] = att.astype(BF16)


def weight_part_body(parts, keep_ref, other_ref, dy_ref, dy_other_ref, *outs):
    me = lax.axis_index("ctx")
    cols = dy_ref.shape[1] // parts
    left = jnp.concatenate([keep_ref[...], other_ref[...]], 1)
    for m, out in enumerate(outs):
        at = pl.ds(pl.multiple_of((me ^ m) * cols, cols), cols)
        right = jnp.concatenate([dy_ref[:, at], dy_other_ref[:, at]], 0)
        out[...] = dot(left, right, NN).astype(out.dtype)


def weight_plane_body(count, *refs):
    ins, outs = refs[:count], refs[count:]
    me = lax.axis_index("dp") // 2
    rows = outs[0].shape[0]
    for m, out in enumerate(outs):
        at = pl.ds(pl.multiple_of((me ^ m) * rows, rows), rows)
        total = ins[0][at, :].astype(F32)
        for r in ins[1:]:
            total = total + r[at, :].astype(F32)
        out[...] = total.astype(out.dtype)


def weight_sum_body(factor, *refs):
    total = refs[0][...].astype(F32)
    for r in refs[1:-1]:
        total = total + r[...].astype(F32)
    refs[-1][...] = total * factor


def head_at(h):
    start = h * HEAD_WIDTH
    return pl.ds(start if isinstance(h, int) else pl.multiple_of(start, HEAD_WIDTH), HEAD_WIDTH)


def lanes_at(start):
    return pl.ds(start if isinstance(start, int) else pl.multiple_of(start, HEAD_WIDTH), HEAD_WIDTH)


def band_of(refs, tokens, start):
    return jnp.concatenate([r[:tokens, lanes_at(start)] for r in refs], 0)


def heads_backward(place, js, q_ref, band, dy_ref, probs, attfs, pieces, ds_ref, first):
    head, group = place()
    tokens = q_ref.shape[0]
    width = band[0].shape[1] // 2
    values = band_of(band, tokens, width + group(js[0]) * HEAD_WIDTH)
    prob_list, d_rows, q_rows = [], [], []
    for i, (j, piece) in enumerate(zip(js, pieces)):
        at = head_at(head(j) // 2)
        dat = dot(piece[...], dy_ref[...], NT).astype(BF16)
        delta = (dat.astype(F32) * attfs[j % 2][at, :]).sum(axis=0, keepdims=True)
        prob = probs[j % 2][:, at]
        ds_ref[:, head_at(first + i)] = (prob.astype(F32) * (dot(values, dat, NN) - delta)).astype(BF16)
        prob_list.append(prob)
        d_rows.append(dat.T)
        q_rows.append(q_ref[:, head_at(head(j))])
    ds = ds_ref[:, first * HEAD_WIDTH : (first + len(js)) * HEAD_WIDTH]
    part_k = dot(ds, jnp.concatenate(q_rows, 0), NN)
    part_v = dot(jnp.concatenate(prob_list, 1), jnp.concatenate(d_rows, 0), NN)
    return part_k, part_v


def backward_first_body(scale, place, q_ref, prev_ref, own_ref, next_ref, dy_ref, p0, p1, a0, a1, *rest):
    pieces, (whole_ref, half_ref, ds_ref) = rest[:6], rest[6:]
    shared = (q_ref, (prev_ref, own_ref, next_ref), dy_ref, (p0, p1), (a0, a1))
    part_k, part_v = heads_backward(place, range(4), *shared, pieces[:4], ds_ref, 0)
    whole_ref[:, :HEAD_WIDTH] = (part_k * scale).astype(BF16)
    whole_ref[:, HEAD_WIDTH:] = part_v.astype(BF16)
    part_k, part_v = heads_backward(place, (4, 5), *shared, pieces[4:], ds_ref, 4)
    half_ref[:, :HEAD_WIDTH] = part_k
    half_ref[:, HEAD_WIDTH:] = part_v


def backward_second_body(scale, place, q_ref, prev_ref, own_ref, next_ref, dy_ref, p0, p1, a0, a1, *rest):
    pieces, whole_ref, half_ref = rest[:2], rest[2], rest[3]
    outs, ds_ref = rest[4:7], rest[7]
    _, group = place()
    tokens = q_ref.shape[0]
    width = own_ref.shape[1] // 2
    shared = (q_ref, (prev_ref, own_ref, next_ref), dy_ref, (p0, p1), (a0, a1))
    part_k, part_v = heads_backward(place, (6, 7), *shared, pieces, ds_ref, 0)
    part_k = ((part_k + half_ref[:, :HEAD_WIDTH]) * scale).astype(BF16)
    part_v = (part_v + half_ref[:, HEAD_WIDTH:]).astype(BF16)
    for t, out in enumerate(outs):
        rows = slice(t * tokens, (t + 1) * tokens)
        out[:, lanes_at(group(6) * HEAD_WIDTH)] = part_k[rows]
        out[:, lanes_at(width + group(6) * HEAD_WIDTH)] = part_v[rows]
        out[:, lanes_at(group(0) * HEAD_WIDTH)] = whole_ref[rows, :HEAD_WIDTH]
        out[:, lanes_at(width + group(0) * HEAD_WIDTH)] = whole_ref[rows, HEAD_WIDTH:]


def output_body(scale, place, prev_ref, own_ref, next_ref, ds_ref, ds_last_ref, t0, t1, *rest):
    pieces, (mixed_ref, gq_ref) = rest[:QUERY_HEADS], rest[QUERY_HEADS:]
    head, group = place()
    tokens = mixed_ref.shape[0]
    ds = (ds_ref[:, : 4 * HEAD_WIDTH], jnp.concatenate([ds_ref[:, 4 * HEAD_WIDTH :], ds_last_ref[...]], 1))
    for half in range(2):
        keys = band_of((prev_ref, own_ref, next_ref), tokens, group(4 * half) * HEAD_WIDTH)
        dq = dot(keys.T, ds[half], NN) * scale
        for i in range(4):
            gq_ref[:, head_at(head(4 * half + i))] = dq[:, i * tokens : (i + 1) * tokens].T.astype(BF16)
    total = jnp.zeros(mixed_ref.shape, F32)
    for j in range(0, QUERY_HEADS, 2):
        at = head_at(head(j) // 2)
        att = jnp.concatenate([t0[at, :].T, t1[at, :].T], 1)
        total = total + dot(att, jnp.concatenate([pieces[j][...], pieces[j + 1][...]], 0), NN)
    mixed_ref[...] = total.astype(BF16)


def key_value_body(own_ref, low_ref, high_ref, gk_ref, gv_ref):
    width = gk_ref.shape[1]
    total = own_ref[...].astype(F32) + low_ref[...].astype(F32) + high_ref[...].astype(F32)
    gk_ref[...] = total[:, :width].astype(BF16)
    gv_ref[...] = total[:, width:].astype(BF16)


def power_of_two(n):
    return n & (n - 1) == 0


def flip(value, axis, mask):
    return lax.ppermute(value, axis, [(i, i ^ mask) for i in range(lax.axis_size(axis))])


def turn(value, axis, step):
    count = lax.axis_size(axis)
    return lax.ppermute(value, axis, [(i, (i + step) % count) for i in range(count)])


def sublayer(queries, keys_in, values_in, patch_order, block_mask, out_weight, cotangent):
    scale = 1.0 / math.sqrt(HEAD_WIDTH)
    n_dp, n_ctx = lax.axis_size("dp"), lax.axis_size("ctx")
    q, k, v, dy = queries[0], keys_in[0], values_in[0], cotangent[0]
    tokens, query_width = q.shape
    kv_width = k.shape[1]
    model = dy.shape[1]
    band = 3 * tokens
    by_head = n_dp == QUERY_HEADS
    column_width = model // n_ctx
    staged = by_head and power_of_two(n_ctx) and column_width % 128 == 0
    macs = tokens * query_width
    group_heads = QUERY_HEADS // KEY_VALUE_HEADS

    own = call(
        pack_body,
        [shape((tokens + HALO_ROWS, 2 * kv_width))],
        [hbm()] * 3,
        in_hbm(k, v, patch_order[0]),
        scratch=[pltpu.VMEM((1, tokens), jnp.int32), pltpu.SemaphoreType.DMA((3,))],
        room=16<<20,
    )[0]
    dy_hbm = dy
    mask = block_mask[0]
    q, dy, table = call(
        fetch_body,
        [shape(q.shape), shape(dy.shape), shape((mask.shape[1] * HALO_ROWS, tokens), F32)],
        [hbm()] * 3,
        in_hbm(q, dy, mask),
        scratch=[pltpu.SMEM(mask.shape, jnp.int32), pltpu.SemaphoreType.DMA((3,))],
    )
    prev_kv = turn(own, "ctx", 1)
    next_kv = turn(own, "ctx", -1)

    if by_head:
        mine = {0: out_weight}
        for j in range(n_dp // 2, 1, -2):
            mine[j] = flip(out_weight, "dp", j)
        for j in range(n_dp // 2 + 2, n_dp, 2):
            mine[j] = flip(mine[n_dp // 2], "dp", j - n_dp // 2)

        def place():
            me = lax.axis_index("dp")
            return (lambda j: me ^ j), (lambda j: (me ^ j) // group_heads)
    else:
        weight_all = lax.all_gather(out_weight, "dp", axis=0, tiled=True)
        pieces = [weight_all.reshape(QUERY_HEADS, HEAD_WIDTH, model)[h] for h in range(QUERY_HEADS)]

        def place():
            return (lambda j: j), (lambda j: j // group_heads)

    half = query_width // 2
    prob, attf, att = [], [], []
    for side in (1, 0):
        done = call(
            functools.partial(forward_body, scale, place, side),
            [shape((band, half)), shape((half, tokens), F32), shape((half, tokens))],
            [vmem()] * 5,
            (q, prev_kv, own, next_kv, table),
            flops=2 * macs * band,
        )
        for held, new in zip((prob, attf, att), done):
            held.insert(0, new)

    total_tokens = n_dp * tokens * n_ctx
    norm_factor = 1.0 / math.sqrt(total_tokens)
    if staged:
        dy_other = flip(dy_hbm, "dp", 1)
        other = flip(att[1], "dp", 1)
        parts = call(
            functools.partial(weight_part_body, n_ctx),
            [shape((half, column_width))] * n_ctx,
            [vmem()] * 4,
            (att[0], other, dy, dy_other),
            flops=2 * half * 2 * tokens * model,
        )
        arrived = [parts[0]]
        for m in range(1, n_ctx):
            arrived.append(flip(parts[m], "ctx", m))
        n_z = n_dp // 2
        blocks = call(
            functools.partial(weight_plane_body, n_ctx),
            [shape((half // n_z, column_width))] * n_z,
            [vmem()] * n_ctx,
            arrived,
        )
        landed = [blocks[0]]
        for m in range(1, n_z):
            landed.append(flip(blocks[m], "dp", 2 * m))
        grad_weight = call(
            functools.partial(weight_sum_body, norm_factor),
            [shape((half // n_z, column_width), F32)],
            [vmem()] * n_z,
            landed,
        )[0]
    else:
        by_pair = jnp.stack([a.reshape(PAIRS, HEAD_WIDTH, tokens) for a in att], 1)
        part = dot(by_pair.reshape(query_width, tokens), dy, NN).astype(BF16)
        columns = lax.psum_scatter(part, "ctx", scatter_dimension=1, tiled=True).astype(F32)
        grad_weight = lax.psum_scatter(columns, "dp", scatter_dimension=0, tiled=True) * norm_factor

    if by_head:
        pieces = []
        for j in range(0, n_dp, 2):
            pieces += [mine[j], flip(mine[j], "dp", 1)]

    whole, half_sum, ds = call(
        functools.partial(backward_first_body, scale, place),
        [shape((band, 2 * HEAD_WIDTH)), shape((band, 2 * HEAD_WIDTH), F32), shape((band, 6 * HEAD_WIDTH))],
        [vmem()] * 15,
        (q, prev_kv, own, next_kv, dy, *prob, *attf, *pieces[:6]),
        flops=(2 * macs * model + 6 * macs * band) * 3 // 4,
    )
    low, mid, high, ds_last = call(
        functools.partial(backward_second_body, scale, place),
        [shape((tokens, 2 * kv_width))] * 3 + [shape((band, 2 * HEAD_WIDTH))],
        [vmem()] * 13,
        (q, prev_kv, own, next_kv, dy, *prob, *attf, *pieces[6:], whole, half_sum),
        flops=(2 * macs * model + 6 * macs * band) // 4,
    )
    from_next = turn(low, "ctx", -1)
    from_prev = turn(high, "ctx", 1)
    mixed, grad_q = call(
        functools.partial(output_body, scale, place),
        [shape((tokens, model)), shape((tokens, query_width))],
        [vmem()] * 15,
        (prev_kv, own, next_kv, ds, ds_last, *att, *pieces),
        flops=2 * macs * model + 2 * macs * band,
    )
    grad_k, grad_v = call(key_value_body, [shape((tokens, kv_width))] * 2, [vmem()] * 3, (mid, from_next, from_prev))
    return (mixed[None], grad_q[None], grad_k[None], grad_v[None], grad_weight)


def solution(mesh):
    row = P("dp", "ctx", None)
    in_specs = (row, row, row, row, row, P("dp", None), row)
    out_specs = (row, row, row, row, P("dp", "ctx"))
    return jax.shard_map(sublayer, mesh=mesh, in_specs=in_specs, out_specs=out_specs, check_vma=False)
```

profile of v0, /device:TPU:0, one launch (start us, length us, event | category | flops | bytes accessed | tf_op | source)
XLA Modules:
  0.0 55.4 jit_solution(16647522430944045546)
XLA Ops:
  0.6 0.0 copy-start
  0.6 4.1 %collective-permute-start.5 = (bf16[128,1024]{1,0:T(8,128)(2,1)}, bf16[128,1024]{1,0:T(8,128)(2,1)S(1)}, u32[]{:S(2)}, u32[]{:S(2)}) collective-permute-start(bf16[128,1024]{1,0:T(8,128)(2,1)} %rest_0_.3), channel_id=1, source_target_pairs={{0,4},{1,5},{2,6},{3,7},{4,0},{5,1},{6,2},{7,3},{8,12},{9,13},{10,... | collective-permute-start | bytes 786440 | tf_op jit(solution)/shard_map/ppermute | solution.py:258
  4.8 1.6 %collective-permute-start.3 = (bf16[128,1024]{1,0:T(8,128)(2,1)}, bf16[128,1024]{1,0:T(8,128)(2,1)S(1)}, u32[]{:S(2)}, u32[]{:S(2)}) collective-permute-start(bf16[128,1024]{1,0:T(8,128)(2,1)} %rest_0_.3), channel_id=1, source_target_pairs={{0,2},{1,3},{2,0},{3,1},{4,6},{5,7},{6,4},{7,5},{8,10},{9,11},{10,... | collective-permute-start | bytes 786440 | tf_op jit(solution)/shard_map/ppermute | solution.py:258
  6.3 0.9 %shard_map.110.own_ref = bf16[136,512]{1,0:T(8,128)(2,1)S(1)} custom-call(bf16[128,256]{1,0:T(8,128)(2,1)} %bitcast.13, bf16[128,256]{1,0:T(8,128)(2,1)} %bitcast.14, s32[1,128]{1,0:T(1,128)} %bitcast.16), custom_call_target="tpu_custom_call" | custom-call | flops 1048576 | bytes 270848 | tf_op jit(solution)/shard_map/pallas_call | solution.py:44
  7.3 1.5 %collective-permute-start = (bf16[136,512]{1,0:T(8,128)(2,1)S(1)}, bf16[136,512]{1,0:T(8,128)(2,1)S(1)}, u32[]{:S(2)}, u32[]{:S(2)}) collective-permute-start(bf16[136,512]{1,0:T(8,128)(2,1)S(1)} %shard_map.110.own_ref), channel_id=1, source_target_pairs={{0,8},{8,16},{16,24},{24,0},{1,9},{9,17},{17,25},{25,1},{2,10},{10... | collective-permute-start | bytes 417800 | tf_op jit(solution)/shard_map/ppermute | solution.py:263
  8.8 0.0 collective-permute-start.12
  8.8 8.2 %collective-permute-done.5.rest_4_ = bf16[128,1024]{1,0:T(8,128)(2,1)S(1)} collective-permute-done((bf16[128,1024]{1,0:T(8,128)(2,1)}, bf16[128,1024]{1,0:T(8,128)(2,1)S(1)}, u32[]{:S(2)}, u32[]{:S(2)}) %collective-permute-start.5) | collective-permute-done | bytes 262176 | tf_op jit(solution)/shard_map/ppermute | solution.py:258
  17.0 0.7 %collective-permute-start.7 = (bf16[128,1024]{1,0:T(8,128)(2,1)S(1)}, bf16[128,1024]{1,0:T(8,128)(2,1)S(1)}, u32[]{:S(2)}, u32[]{:S(2)}) collective-permute-start(bf16[128,1024]{1,0:T(8,128)(2,1)S(1)} %collective-permute-done.5.rest_4_), channel_id=1, source_target_pairs={{0,2},{1,3},{2,0},{3,1},{4,6},{5,7},{6,4},{7,5},{8,10},{9,11},{10,... | collective-permute-start | bytes 786440 | tf_op jit(solution)/shard_map/ppermute | solution.py:258
  17.7 2.4 %collective-permute-start.1 = (bf16[136,512]{1,0:T(8,128)(2,1)S(1)}, bf16[136,512]{1,0:T(8,128)(2,1)S(1)}, u32[]{:S(2)}, u32[]{:S(2)}) collective-permute-start(bf16[136,512]{1,0:T(8,128)(2,1)S(1)} %shard_map.110.own_ref), channel_id=1, source_target_pairs={{0,24},{8,0},{16,8},{24,16},{1,25},{9,1},{17,9},{25,17},{2,26},{10... | collective-permute-start | bytes 417800 | tf_op jit(solution)/shard_map/ppermute | solution.py:263
  20.2 0.0 collective-permute-done.prev_ref
  20.2 0.0 copy-done
  20.2 0.0 collective-permute-start.2
  20.2 0.0 collective-permute-done.3.rest_2_
  20.2 0.5 collective-permute-start.4
  20.7 1.1 %shard_map.111 = (bf16[128,1024]{1,0:T(8,128)(2,1)S(1)}, bf16[128,1024]{1,0:T(8,128)(2,1)S(1)}, f32[64,128]{1,0:T(8,128)S(1)}) custom-call(bf16[128,1024]{1,0:T(8,128)(2,1)} %bitcast.10, bf16[128,1024]{1,0:T(8,128)(2,1)} %bitcast.12, s32[4,8]{1,0:T(4,128)} %bitcast.15), custom_call_target="tpu_custom_call" | custom-call | flops 1048576 | bytes 1081472 | tf_op jit(solution)/shard_map/pallas_call | solution.py:44
  21.8 1.3 %collective-permute-done.1.next_ref = bf16[136,512]{1,0:T(8,128)(2,1)S(1)} collective-permute-done((bf16[136,512]{1,0:T(8,128)(2,1)S(1)}, bf16[136,512]{1,0:T(8,128)(2,1)S(1)}, u32[]{:S(2)}, u32[]{:S(2)}) %collective-permute-start.1) | collective-permute-done | bytes 139296 | tf_op jit(solution)/shard_map/ppermute | solution.py:263
  23.1 0.7 %shard_map.113 = (bf16[384,512]{1,0:T(8,128)(2,1)S(1)}, f32[512,128]{1,0:T(8,128)S(1)}, bf16[512,128]{1,0:T(8,128)(2,1)S(1)}) custom-call(bf16[128,1024]{1,0:T(8,128)(2,1)S(1)} %get-tuple-element.33.q_ref, bf16[136,512]{1,0:T(8,128)(2,1)S(1)} %collective-permute-done.prev_ref, bf16[136,512]{1,0:T(8,128)(2,1)S(1)} %shard_map.110.own_ref, ...), custom_call_target="tpu_custom_call" | custom-call | flops 100663296 | bytes 1499136 | tf_op jit(solution)/shard_map/pallas_call | solution.py:44
  23.8 0.1 collective-permute-start.11
  23.9 0.0 collective-permute-done.12.dy_other_ref
  23.9 0.5 collective-permute-start.6
  24.4 0.1 collective-permute-done.7.rest_0_.rest_6_
  24.4 0.0 collective-permute-start.8
  24.5 0.7 %shard_map.112 = (bf16[384,512]{1,0:T(8,128)(2,1)S(1)}, f32[512,128]{1,0:T(8,128)S(1)}, bf16[512,128]{1,0:T(8,128)(2,1)S(1)}) custom-call(bf16[128,1024]{1,0:T(8,128)(2,1)S(1)} %get-tuple-element.33.q_ref, bf16[136,512]{1,0:T(8,128)(2,1)S(1)} %collective-permute-done.prev_ref, bf16[136,512]{1,0:T(8,128)(2,1)S(1)} %shard_map.110.own_ref, ...), custom_call_target="tpu_custom_call" | custom-call | flops 100663296 | bytes 1499136 | tf_op jit(solution)/shard_map/pallas_call | solution.py:44
  25.2 0.0 collective-permute-done.11.other_ref
  25.2 0.5 shard_map.118
  25.7 2.5 %collective-permute-start.13 = (bf16[512,256]{1,0:T(8,128)(2,1)S(1)}, bf16[512,256]{1,0:T(8,128)(2,1)S(1)}, u32[]{:S(2)}, u32[]{:S(2)}) collective-permute-start(bf16[512,256]{1,0:T(8,128)(2,1)S(1)} %get-tuple-element.54), channel_id=1, source_target_pairs={{0,8},{8,0},{16,24},{24,16},{1,9},{9,1},{17,25},{25,17},{2,10},{10... | collective-permute-start | bytes 786440 | tf_op jit(solution)/shard_map/ppermute | solution.py:258
  28.1 0.0 collective-permute-done.2.rest_1_
  28.1 1.5 %collective-permute-start.14 = (bf16[512,256]{1,0:T(8,128)(2,1)S(1)}, bf16[512,256]{1,0:T(8,128)(2,1)S(1)}, u32[]{:S(2)}, u32[]{:S(2)}) collective-permute-start(bf16[512,256]{1,0:T(8,128)(2,1)S(1)} %get-tuple-element.55), channel_id=1, source_target_pairs={{0,16},{8,24},{16,0},{24,8},{1,17},{9,25},{17,1},{25,9},{2,18},{10... | collective-permute-start | bytes 786440 | tf_op jit(solution)/shard_map/ppermute | solution.py:258
  29.7 0.0 collective-permute-done.4.rest_3_
  29.7 0.0 collective-permute-start.15
  29.7 0.0 collective-permute-done.6.rest_5_
  29.7 2.2 %shard_map.114 = (bf16[384,256]{1,0:T(8,128)(2,1)S(1)}, f32[384,256]{1,0:T(8,128)S(1)}, bf16[384,768]{1,0:T(8,128)(2,1)S(1)}) custom-call(bf16[128,1024]{1,0:T(8,128)(2,1)S(1)} %get-tuple-element.33.q_ref, bf16[136,512]{1,0:T(8,128)(2,1)S(1)} %collective-permute-done.prev_ref, bf16[136,512]{1,0:T(8,128)(2,1)S(1)} %shard_map.110.own_ref, ...), custom_call_target="tpu_custom_call" | custom-call | flops 427819008 | bytes 5005312 | tf_op jit(solution)/shard_map/pallas_call | solution.py:44
  31.9 0.0 collective-permute-done.8.rest_1_.rest_7_
  31.9 1.0 %shard_map.115 = (bf16[128,512]{1,0:T(8,128)(2,1)S(1)}, bf16[128,512]{1,0:T(8,128)(2,1)S(1)}, bf16[128,512]{1,0:T(8,128)(2,1)S(1)}, bf16[384,256]{1,0:T(8,128)(2,1)S(1)}) custom-call(bf16[128,1024]{1,0:T(8,128)(2,1)S(1)} %get-tuple-element.33.q_ref, bf16[136,512]{1,0:T(8,128)(2,1)S(1)} %collective-permute-done.prev_ref, ...), custom_call_target="tpu_custom_call" | custom-call | flops 142606336 | bytes 3956736 | tf_op jit(solution)/shard_map/pallas_call | solution.py:44
  32.9 2.9 %collective-permute-start.9 = (bf16[128,512]{1,0:T(8,128)(2,1)S(1)}, bf16[128,512]{1,0:T(8,128)(2,1)S(1)}, u32[]{:S(2)}, u32[]{:S(2)}) collective-permute-start(bf16[128,512]{1,0:T(8,128)(2,1)S(1)} %get-tuple-element.49), channel_id=1, source_target_pairs={{0,24},{8,0},{16,8},{24,16},{1,25},{9,1},{17,9},{25,17},{2,26},{10... | collective-permute-start | bytes 393224 | tf_op jit(solution)/shard_map/ppermute | solution.py:263
  35.9 0.0 collective-permute-start.10
  35.9 0.0 collective-permute-done.13.refs_1_
  35.9 6.2 %collective-permute-done.14.refs_2_ = bf16[512,256]{1,0:T(8,128)(2,1)S(1)} collective-permute-done((bf16[512,256]{1,0:T(8,128)(2,1)S(1)}, bf16[512,256]{1,0:T(8,128)(2,1)S(1)}, u32[]{:S(2)}, u32[]{:S(2)}) %collective-permute-start.14) | collective-permute-done | bytes 262176 | tf_op jit(solution)/shard_map/ppermute | solution.py:258
  42.1 0.0 collective-permute-done.15.refs_3_
  42.1 0.1 shard_map.119
  42.3 1.2 %collective-permute-start.16 = (bf16[128,256]{1,0:T(8,128)(2,1)S(1)}, bf16[128,256]{1,0:T(8,128)(2,1)S(1)}, u32[]{:S(2)}, u32[]{:S(2)}) collective-permute-start(bf16[128,256]{1,0:T(8,128)(2,1)S(1)} %get-tuple-element.58), channel_id=1, source_target_pairs={{0,2},{1,3},{2,0},{3,1},{4,6},{5,7},{6,4},{7,5},{8,10},{9,11},{10,... | collective-permute-start | bytes 196616 | tf_op jit(solution)/shard_map/ppermute | solution.py:258
  43.4 3.1 %collective-permute-start.17 = (bf16[128,256]{1,0:T(8,128)(2,1)S(1)}, bf16[128,256]{1,0:T(8,128)(2,1)S(1)}, u32[]{:S(2)}, u32[]{:S(2)}) collective-permute-start(bf16[128,256]{1,0:T(8,128)(2,1)S(1)} %get-tuple-element.59), channel_id=1, source_target_pairs={{0,4},{1,5},{2,6},{3,7},{4,0},{5,1},{6,2},{7,3},{8,12},{9,13},{10,... | collective-permute-start | bytes 196616 | tf_op jit(solution)/shard_map/ppermute | solution.py:258
  46.5 0.5 collective-permute-start.18
  47.1 0.2 collective-permute-done.16.refs_1_
  47.3 3.9 %collective-permute-done.17.refs_2_ = bf16[128,256]{1,0:T(8,128)(2,1)S(1)} collective-permute-done((bf16[128,256]{1,0:T(8,128)(2,1)S(1)}, bf16[128,256]{1,0:T(8,128)(2,1)S(1)}, u32[]{:S(2)}, u32[]{:S(2)}) %collective-permute-start.17) | collective-permute-done | bytes 65568 | tf_op jit(solution)/shard_map/ppermute | solution.py:258
  51.1 1.5 %collective-permute-done.18.refs_3_ = bf16[128,256]{1,0:T(8,128)(2,1)S(1)} collective-permute-done((bf16[128,256]{1,0:T(8,128)(2,1)S(1)}, bf16[128,256]{1,0:T(8,128)(2,1)S(1)}, u32[]{:S(2)}, u32[]{:S(2)}) %collective-permute-start.18) | collective-permute-done | bytes 65568 | tf_op jit(solution)/shard_map/ppermute | solution.py:258
  52.6 0.7 %shard_map.120 = f32[128,256]{1,0:T(8,128)} custom-call(bf16[128,256]{1,0:T(8,128)(2,1)S(1)} %get-tuple-element.57.refs_0_, bf16[128,256]{1,0:T(8,128)(2,1)S(1)} %collective-permute-done.16.refs_1_, bf16[128,256]{1,0:T(8,128)(2,1)S(1)} %collective-permute-done.17.refs_2_, bf16[128,256]{1,0:T(8,128)(2,1)S(1)} %collective-permute-done.18.refs_3_), custom_call_target="tpu_custom_call" | custom-call | flops 1048576 | bytes 393216 | tf_op jit(solution)/shard_map/pallas_call | solution.py:44
  53.3 1.3 %shard_map.116 = (bf16[128,1024]{1,0:T(8,128)(2,1)}, bf16[128,1024]{1,0:T(8,128)(2,1)}) custom-call(bf16[136,512]{1,0:T(8,128)(2,1)S(1)} %collective-permute-done.prev_ref, bf16[136,512]{1,0:T(8,128)(2,1)S(1)} %shard_map.110.own_ref, bf16[136,512]{1,0:T(8,128)(2,1)S(1)} %collective-permute-done.1.next_ref, bf16[384,768]{1,0:T(8,128)(2,1)S(1)} %get-tuple-element.40.ds_ref, ...), custom_call_target="tpu_custom_call" | custom-call | flops 369098752 | bytes 4087808 | tf_op jit(solution)/shard_map/pallas_call | solution.py:44
  54.7 0.0 collective-permute-done.9.low_ref
  54.7 0.0 collective-permute-done.10.high_ref
  54.7 0.7 %shard_map.117 = (bf16[128,256]{1,0:T(8,128)(2,1)}, bf16[128,256]{1,0:T(8,128)(2,1)}) custom-call(bf16[128,512]{1,0:T(8,128)(2,1)S(1)} %get-tuple-element.48.own_ref, bf16[128,512]{1,0:T(8,128)(2,1)S(1)} %collective-permute-done.9.low_ref, bf16[128,512]{1,0:T(8,128)(2,1)S(1)} %collective-permute-done.10.high_ref), custom_call_target="tpu_custom_call" | custom-call | flops 1048576 | bytes 524288 | tf_op jit(solution)/shard_map/pallas_call | solution.py:44
Async XLA Ops:
  0.6 19.6 %copy-start = (bf16[128,1024]{1,0:T(8,128)(2,1)S(1)}, bf16[128,1024]{1,0:T(8,128)(2,1)}, u32[]{:S(2)}) copy-start(bf16[128,1024]{1,0:T(8,128)(2,1)} %rest_0_.3) | copy-start | bytes 786436
  0.6 16.4 %collective-permute-start.5 = (bf16[128,1024]{1,0:T(8,128)(2,1)}, bf16[128,1024]{1,0:T(8,128)(2,1)S(1)}, u32[]{:S(2)}, u32[]{:S(2)}) collective-permute-start(bf16[128,1024]{1,0:T(8,128)(2,1)} %rest_0_.3), channel_id=1, source_target_pairs={{0,4},{1,5},{2,6},{3,7},{4,0},{5,1},{6,2},{7,3},{8,12},{9,13},{10,... | collective-permute-start | bytes 786440 | tf_op jit(solution)/shard_map/ppermute | solution.py:258
  4.8 15.4 %collective-permute-start.3 = (bf16[128,1024]{1,0:T(8,128)(2,1)}, bf16[128,1024]{1,0:T(8,128)(2,1)S(1)}, u32[]{:S(2)}, u32[]{:S(2)}) collective-permute-start(bf16[128,1024]{1,0:T(8,128)(2,1)} %rest_0_.3), channel_id=1, source_target_pairs={{0,2},{1,3},{2,0},{3,1},{4,6},{5,7},{6,4},{7,5},{8,10},{9,11},{10,... | collective-permute-start | bytes 786440 | tf_op jit(solution)/shard_map/ppermute | solution.py:258
  7.3 12.9 %collective-permute-start = (bf16[136,512]{1,0:T(8,128)(2,1)S(1)}, bf16[136,512]{1,0:T(8,128)(2,1)S(1)}, u32[]{:S(2)}, u32[]{:S(2)}) collective-permute-start(bf16[136,512]{1,0:T(8,128)(2,1)S(1)} %shard_map.110.own_ref), channel_id=1, source_target_pairs={{0,8},{8,16},{16,24},{24,0},{1,9},{9,17},{17,25},{25,1},{2,10},{10... | collective-permute-start | bytes 417800 | tf_op jit(solution)/shard_map/ppermute | solution.py:263
  8.8 15.1 %collective-permute-start.12 = (bf16[128,1024]{1,0:T(8,128)(2,1)}, bf16[128,1024]{1,0:T(8,128)(2,1)S(1)}, u32[]{:S(2)}, u32[]{:S(2)}) collective-permute-start(bf16[128,1024]{1,0:T(8,128)(2,1)} %bitcast.11), channel_id=1, source_target_pairs={{0,1},{1,0},{2,3},{3,2},{4,5},{5,4},{6,7},{7,6},{8,9},{9,8},{10,11... | collective-permute-start | bytes 786440 | tf_op jit(solution)/shard_map/ppermute | solution.py:258
  17.0 7.4 %collective-permute-start.7 = (bf16[128,1024]{1,0:T(8,128)(2,1)S(1)}, bf16[128,1024]{1,0:T(8,128)(2,1)S(1)}, u32[]{:S(2)}, u32[]{:S(2)}) collective-permute-start(bf16[128,1024]{1,0:T(8,128)(2,1)S(1)} %collective-permute-done.5.rest_4_), channel_id=1, source_target_pairs={{0,2},{1,3},{2,0},{3,1},{4,6},{5,7},{6,4},{7,5},{8,10},{9,11},{10,... | collective-permute-start | bytes 786440 | tf_op jit(solution)/shard_map/ppermute | solution.py:258
  17.7 5.3 %collective-permute-start.1 = (bf16[136,512]{1,0:T(8,128)(2,1)S(1)}, bf16[136,512]{1,0:T(8,128)(2,1)S(1)}, u32[]{:S(2)}, u32[]{:S(2)}) collective-permute-start(bf16[136,512]{1,0:T(8,128)(2,1)S(1)} %shard_map.110.own_ref), channel_id=1, source_target_pairs={{0,24},{8,0},{16,8},{24,16},{1,25},{9,1},{17,9},{25,17},{2,26},{10... | collective-permute-start | bytes 417800 | tf_op jit(solution)/shard_map/ppermute | solution.py:263
  20.2 8.0 %collective-permute-start.2 = (bf16[128,1024]{1,0:T(8,128)(2,1)S(1)}, bf16[128,1024]{1,0:T(8,128)(2,1)S(1)}, u32[]{:S(2)}, u32[]{:S(2)}) collective-permute-start(bf16[128,1024]{1,0:T(8,128)(2,1)S(1)} %copy-done), channel_id=1, source_target_pairs={{0,1},{1,0},{2,3},{3,2},{4,5},{5,4},{6,7},{7,6},{8,9},{9,8},{10,11... | collective-permute-start | bytes 786440 | tf_op jit(solution)/shard_map/ppermute | solution.py:258
  20.2 9.5 %collective-permute-start.4 = (bf16[128,1024]{1,0:T(8,128)(2,1)S(1)}, bf16[128,1024]{1,0:T(8,128)(2,1)S(1)}, u32[]{:S(2)}, u32[]{:S(2)}) collective-permute-start(bf16[128,1024]{1,0:T(8,128)(2,1)S(1)} %collective-permute-done.3.rest_2_), channel_id=1, source_target_pairs={{0,1},{1,0},{2,3},{3,2},{4,5},{5,4},{6,7},{7,6},{8,9},{9,8},{10,11... | collective-permute-start | bytes 786440 | tf_op jit(solution)/shard_map/ppermute | solution.py:258
  23.8 1.4 %collective-permute-start.11 = (bf16[512,128]{1,0:T(8,128)(2,1)S(1)}, bf16[512,128]{1,0:T(8,128)(2,1)S(1)}, u32[]{:S(2)}, u32[]{:S(2)}) collective-permute-start(bf16[512,128]{1,0:T(8,128)(2,1)S(1)} %get-tuple-element.45.t1), channel_id=1, source_target_pairs={{0,1},{1,0},{2,3},{3,2},{4,5},{5,4},{6,7},{7,6},{8,9},{9,8},{10,11... | collective-permute-start | bytes 393224 | tf_op jit(solution)/shard_map/ppermute | solution.py:258
  23.9 5.8 %collective-permute-start.6 = (bf16[128,1024]{1,0:T(8,128)(2,1)S(1)}, bf16[128,1024]{1,0:T(8,128)(2,1)S(1)}, u32[]{:S(2)}, u32[]{:S(2)}) collective-permute-start(bf16[128,1024]{1,0:T(8,128)(2,1)S(1)} %collective-permute-done.5.rest_4_), channel_id=1, source_target_pairs={{0,1},{1,0},{2,3},{3,2},{4,5},{5,4},{6,7},{7,6},{8,9},{9,8},{10,11... | collective-permute-start | bytes 786440 | tf_op jit(solution)/shard_map/ppermute | solution.py:258
  24.4 7.5 %collective-permute-start.8 = (bf16[128,1024]{1,0:T(8,128)(2,1)S(1)}, bf16[128,1024]{1,0:T(8,128)(2,1)S(1)}, u32[]{:S(2)}, u32[]{:S(2)}) collective-permute-start(bf16[128,1024]{1,0:T(8,128)(2,1)S(1)} %collective-permute-done.7.rest_0_.rest_6_), channel_id=1, source_target_pairs={{0,1},{1,0},{2,3},{3,2},{4,5},{5,4},{6,7},{7,6},{8,9},{9,8},{10,11... | collective-permute-start | bytes 786440 | tf_op jit(solution)/shard_map/ppermute | solution.py:258
  25.7 10.2 %collective-permute-start.13 = (bf16[512,256]{1,0:T(8,128)(2,1)S(1)}, bf16[512,256]{1,0:T(8,128)(2,1)S(1)}, u32[]{:S(2)}, u32[]{:S(2)}) collective-permute-start(bf16[512,256]{1,0:T(8,128)(2,1)S(1)} %get-tuple-element.54), channel_id=1, source_target_pairs={{0,8},{8,0},{16,24},{24,16},{1,9},{9,1},{17,25},{25,17},{2,10},{10... | collective-permute-start | bytes 786440 | tf_op jit(solution)/shard_map/ppermute | solution.py:258
  28.1 14.0 %collective-permute-start.14 = (bf16[512,256]{1,0:T(8,128)(2,1)S(1)}, bf16[512,256]{1,0:T(8,128)(2,1)S(1)}, u32[]{:S(2)}, u32[]{:S(2)}) collective-permute-start(bf16[512,256]{1,0:T(8,128)(2,1)S(1)} %get-tuple-element.55), channel_id=1, source_target_pairs={{0,16},{8,24},{16,0},{24,8},{1,17},{9,25},{17,1},{25,9},{2,18},{10... | collective-permute-start | bytes 786440 | tf_op jit(solution)/shard_map/ppermute | solution.py:258
  29.7 12.5 %collective-permute-start.15 = (bf16[512,256]{1,0:T(8,128)(2,1)S(1)}, bf16[512,256]{1,0:T(8,128)(2,1)S(1)}, u32[]{:S(2)}, u32[]{:S(2)}) collective-permute-start(bf16[512,256]{1,0:T(8,128)(2,1)S(1)} %get-tuple-element.56), channel_id=1, source_target_pairs={{0,24},{8,16},{16,8},{24,0},{1,25},{9,17},{17,9},{25,1},{2,26},{10... | collective-permute-start | bytes 786440 | tf_op jit(solution)/shard_map/ppermute | solution.py:258
  32.9 21.7 %collective-permute-start.9 = (bf16[128,512]{1,0:T(8,128)(2,1)S(1)}, bf16[128,512]{1,0:T(8,128)(2,1)S(1)}, u32[]{:S(2)}, u32[]{:S(2)}) collective-permute-start(bf16[128,512]{1,0:T(8,128)(2,1)S(1)} %get-tuple-element.49), channel_id=1, source_target_pairs={{0,24},{8,0},{16,8},{24,16},{1,25},{9,1},{17,9},{25,17},{2,26},{10... | collective-permute-start | bytes 393224 | tf_op jit(solution)/shard_map/ppermute | solution.py:263
  35.9 18.8 %collective-permute-start.10 = (bf16[128,512]{1,0:T(8,128)(2,1)S(1)}, bf16[128,512]{1,0:T(8,128)(2,1)S(1)}, u32[]{:S(2)}, u32[]{:S(2)}) collective-permute-start(bf16[128,512]{1,0:T(8,128)(2,1)S(1)} %get-tuple-element.50), channel_id=1, source_target_pairs={{0,8},{8,16},{16,24},{24,0},{1,9},{9,17},{17,25},{25,1},{2,10},{10... | collective-permute-start | bytes 393224 | tf_op jit(solution)/shard_map/ppermute | solution.py:263
  42.3 5.0 %collective-permute-start.16 = (bf16[128,256]{1,0:T(8,128)(2,1)S(1)}, bf16[128,256]{1,0:T(8,128)(2,1)S(1)}, u32[]{:S(2)}, u32[]{:S(2)}) collective-permute-start(bf16[128,256]{1,0:T(8,128)(2,1)S(1)} %get-tuple-element.58), channel_id=1, source_target_pairs={{0,2},{1,3},{2,0},{3,1},{4,6},{5,7},{6,4},{7,5},{8,10},{9,11},{10,... | collective-permute-start | bytes 196616 | tf_op jit(solution)/shard_map/ppermute | solution.py:258
  43.4 7.7 %collective-permute-start.17 = (bf16[128,256]{1,0:T(8,128)(2,1)S(1)}, bf16[128,256]{1,0:T(8,128)(2,1)S(1)}, u32[]{:S(2)}, u32[]{:S(2)}) collective-permute-start(bf16[128,256]{1,0:T(8,128)(2,1)S(1)} %get-tuple-element.59), channel_id=1, source_target_pairs={{0,4},{1,5},{2,6},{3,7},{4,0},{5,1},{6,2},{7,3},{8,12},{9,13},{10,... | collective-permute-start | bytes 196616 | tf_op jit(solution)/shard_map/ppermute | solution.py:258
  46.5 6.1 %collective-permute-start.18 = (bf16[128,256]{1,0:T(8,128)(2,1)S(1)}, bf16[128,256]{1,0:T(8,128)(2,1)S(1)}, u32[]{:S(2)}, u32[]{:S(2)}) collective-permute-start(bf16[128,256]{1,0:T(8,128)(2,1)S(1)} %get-tuple-element.60), channel_id=1, source_target_pairs={{0,6},{1,7},{2,4},{3,5},{4,2},{5,3},{6,0},{7,1},{8,14},{9,15},{10,... | collective-permute-start | bytes 196616 | tf_op jit(solution)/shard_map/ppermute | solution.py:258
where the time goes:
time: 55.5 us; the launch traced here: 55.4 us
  starting transfers between devices  23.3 us (42%)
  waiting for transfers between devices  21.4 us (39%)
  Pallas kernels  9.94 us (18%)
  between operations  0.76 us (1%)
    ppermute x15, waiting for transfers between devices, flip(): lax.ppermute(value, axis, [(i, i ^ mask) for i in range(lax.axis_size(axi...  20.1 us
    ppermute x15, starting transfers between devices, flip(): lax.ppermute(value, axis, [(i, i ^ mask) for i in range(lax.axis_size(axi...  16.4 us
    pallas_call x11, Pallas kernels, call(): pl.pallas_call(body, out_shape=outs, in_specs=specs, out_specs=[vmem() fo...  9.94 us
    ppermute x4, starting transfers between devices, turn(): lax.ppermute(value, axis, [(i, (i + step) % count) for i in range(count)])  6.94 us
    ppermute x4, waiting for transfers between devices, turn(): lax.ppermute(value, axis, [(i, (i + step) % count) for i in range(count)])  1.29 us
  transfers between devices with their start and end apart: 19, of which 7 were waited for; matrix products, arithmetic and copies ran while one was open for 0% of the time, Pallas kernels for 17%

commit v1 on v0

--- a/solution.py
+++ b/solution.py
@@ -271,9 +271,8 @@
     kv_width = k.shape[1]
     model = dy.shape[1]
     band = 3 * tokens
-    by_head = n_dp == QUERY_HEADS
     column_width = model // n_ctx
-    staged = by_head and power_of_two(n_ctx) and column_width % 128 == 0
+    by_head = n_dp == QUERY_HEADS and power_of_two(n_ctx) and column_width % 128 == 0
     macs = tokens * query_width
     group_heads = QUERY_HEADS // KEY_VALUE_HEADS
 
@@ -329,7 +328,7 @@
 
     total_tokens = n_dp * tokens * n_ctx
     norm_factor = 1.0 / math.sqrt(total_tokens)
-    if staged:
+    if by_head:
         dy_other = flip(dy_hbm, "dp", 1)
         other = flip(att[1], "dp", 1)
         parts = call(

time: 55.5 us -> 55.5 us (level)
  no operation moved by 1% of the time
where the time goes in v1:
time: 55.5 us; the launch traced here: 55.4 us
  starting transfers between devices  23.3 us (42%)
  waiting for transfers between devices  21.4 us (39%)
  Pallas kernels  9.94 us (18%)
  between operations  0.76 us (1%)
    ppermute x15, waiting for transfers between devices, flip(): lax.ppermute(value, axis, [(i, i ^ mask) for i in range(lax.axis_size(axi...  20.1 us
    ppermute x15, starting transfers between devices, flip(): lax.ppermute(value, axis, [(i, i ^ mask) for i in range(lax.axis_size(axi...  16.4 us
    pallas_call x11, Pallas kernels, call(): pl.pallas_call(body, out_shape=outs, in_specs=specs, out_specs=[vmem() fo...  9.94 us
    ppermute x4, starting transfers between devices, turn(): lax.ppermute(value, axis, [(i, (i + step) % count) for i in range(count)])  6.94 us
    ppermute x4, waiting for transfers between devices, turn(): lax.ppermute(value, axis, [(i, (i + step) % count) for i in range(count)])  1.29 us
  transfers between devices with their start and end apart: 19, of which 7 were waited for; matrix products, arithmetic and copies ran while one was open for 0% of the time, Pallas kernels for 17%

profile of v1, /device:TPU:0, one launch (start us, length us, event | category | flops | bytes accessed | tf_op | source)
XLA Modules:
  0.0 55.4 jit_solution(16647522430944045546)
XLA Ops:
  0.6 0.0 copy-start
  0.6 4.1 %collective-permute-start.5 = (bf16[128,1024]{1,0:T(8,128)(2,1)}, bf16[128,1024]{1,0:T(8,128)(2,1)S(1)}, u32[]{:S(2)}, u32[]{:S(2)}) collective-permute-start(bf16[128,1024]{1,0:T(8,128)(2,1)} %rest_0_.3), channel_id=1, source_target_pairs={{0,4},{1,5},{2,6},{3,7},{4,0},{5,1},{6,2},{7,3},{8,12},{9,13},{10,... | collective-permute-start | bytes 786440 | tf_op jit(solution)/shard_map/ppermute | solution.py:258
  4.8 1.6 %collective-permute-start.3 = (bf16[128,1024]{1,0:T(8,128)(2,1)}, bf16[128,1024]{1,0:T(8,128)(2,1)S(1)}, u32[]{:S(2)}, u32[]{:S(2)}) collective-permute-start(bf16[128,1024]{1,0:T(8,128)(2,1)} %rest_0_.3), channel_id=1, source_target_pairs={{0,2},{1,3},{2,0},{3,1},{4,6},{5,7},{6,4},{7,5},{8,10},{9,11},{10,... | collective-permute-start | bytes 786440 | tf_op jit(solution)/shard_map/ppermute | solution.py:258
  6.3 0.9 %shard_map.110.own_ref = bf16[136,512]{1,0:T(8,128)(2,1)S(1)} custom-call(bf16[128,256]{1,0:T(8,128)(2,1)} %bitcast.13, bf16[128,256]{1,0:T(8,128)(2,1)} %bitcast.14, s32[1,128]{1,0:T(1,128)} %bitcast.16), custom_call_target="tpu_custom_call" | custom-call | flops 1048576 | bytes 270848 | tf_op jit(solution)/shard_map/pallas_call | solution.py:44
  7.3 1.5 %collective-permute-start = (bf16[136,512]{1,0:T(8,128)(2,1)S(1)}, bf16[136,512]{1,0:T(8,128)(2,1)S(1)}, u32[]{:S(2)}, u32[]{:S(2)}) collective-permute-start(bf16[136,512]{1,0:T(8,128)(2,1)S(1)} %shard_map.110.own_ref), channel_id=1, source_target_pairs={{0,8},{8,16},{16,24},{24,0},{1,9},{9,17},{17,25},{25,1},{2,10},{10... | collective-permute-start | bytes 417800 | tf_op jit(solution)/shard_map/ppermute | solution.py:263
  8.8 0.0 collective-permute-start.12
  8.8 8.2 %collective-permute-done.5.rest_4_ = bf16[128,1024]{1,0:T(8,128)(2,1)S(1)} collective-permute-done((bf16[128,1024]{1,0:T(8,128)(2,1)}, bf16[128,1024]{1,0:T(8,128)(2,1)S(1)}, u32[]{:S(2)}, u32[]{:S(2)}) %collective-permute-start.5) | collective-permute-done | bytes 262176 | tf_op jit(solution)/shard_map/ppermute | solution.py:258
  17.0 0.7 %collective-permute-start.7 = (bf16[128,1024]{1,0:T(8,128)(2,1)S(1)}, bf16[128,1024]{1,0:T(8,128)(2,1)S(1)}, u32[]{:S(2)}, u32[]{:S(2)}) collective-permute-start(bf16[128,1024]{1,0:T(8,128)(2,1)S(1)} %collective-permute-done.5.rest_4_), channel_id=1, source_target_pairs={{0,2},{1,3},{2,0},{3,1},{4,6},{5,7},{6,4},{7,5},{8,10},{9,11},{10,... | collective-permute-start | bytes 786440 | tf_op jit(solution)/shard_map/ppermute | solution.py:258
  17.7 2.4 %collective-permute-start.1 = (bf16[136,512]{1,0:T(8,128)(2,1)S(1)}, bf16[136,512]{1,0:T(8,128)(2,1)S(1)}, u32[]{:S(2)}, u32[]{:S(2)}) collective-permute-start(bf16[136,512]{1,0:T(8,128)(2,1)S(1)} %shard_map.110.own_ref), channel_id=1, source_target_pairs={{0,24},{8,0},{16,8},{24,16},{1,25},{9,1},{17,9},{25,17},{2,26},{10... | collective-permute-start | bytes 417800 | tf_op jit(solution)/shard_map/ppermute | solution.py:263
  20.2 0.0 collective-permute-done.prev_ref
  20.2 0.0 copy-done
  20.2 0.0 collective-permute-start.2
  20.2 0.0 collective-permute-done.3.rest_2_
  20.2 0.5 collective-permute-start.4
  20.7 1.1 %shard_map.111 = (bf16[128,1024]{1,0:T(8,128)(2,1)S(1)}, bf16[128,1024]{1,0:T(8,128)(2,1)S(1)}, f32[64,128]{1,0:T(8,128)S(1)}) custom-call(bf16[128,1024]{1,0:T(8,128)(2,1)} %bitcast.10, bf16[128,1024]{1,0:T(8,128)(2,1)} %bitcast.12, s32[4,8]{1,0:T(4,128)} %bitcast.15), custom_call_target="tpu_custom_call" | custom-call | flops 1048576 | bytes 1081472 | tf_op jit(solution)/shard_map/pallas_call | solution.py:44
  21.8 1.3 %collective-permute-done.1.next_ref = bf16[136,512]{1,0:T(8,128)(2,1)S(1)} collective-permute-done((bf16[136,512]{1,0:T(8,128)(2,1)S(1)}, bf16[136,512]{1,0:T(8,128)(2,1)S(1)}, u32[]{:S(2)}, u32[]{:S(2)}) %collective-permute-start.1) | collective-permute-done | bytes 139296 | tf_op jit(solution)/shard_map/ppermute | solution.py:263
  23.1 0.7 %shard_map.113 = (bf16[384,512]{1,0:T(8,128)(2,1)S(1)}, f32[512,128]{1,0:T(8,128)S(1)}, bf16[512,128]{1,0:T(8,128)(2,1)S(1)}) custom-call(bf16[128,1024]{1,0:T(8,128)(2,1)S(1)} %get-tuple-element.33.q_ref, bf16[136,512]{1,0:T(8,128)(2,1)S(1)} %collective-permute-done.prev_ref, bf16[136,512]{1,0:T(8,128)(2,1)S(1)} %shard_map.110.own_ref, ...), custom_call_target="tpu_custom_call" | custom-call | flops 100663296 | bytes 1499136 | tf_op jit(solution)/shard_map/pallas_call | solution.py:44
  23.8 0.1 collective-permute-start.11
  23.9 0.0 collective-permute-done.12.dy_other_ref
  23.9 0.5 collective-permute-start.6
  24.4 0.1 collective-permute-done.7.rest_0_.rest_6_
  24.4 0.0 collective-permute-start.8
  24.5 0.7 %shard_map.112 = (bf16[384,512]{1,0:T(8,128)(2,1)S(1)}, f32[512,128]{1,0:T(8,128)S(1)}, bf16[512,128]{1,0:T(8,128)(2,1)S(1)}) custom-call(bf16[128,1024]{1,0:T(8,128)(2,1)S(1)} %get-tuple-element.33.q_ref, bf16[136,512]{1,0:T(8,128)(2,1)S(1)} %collective-permute-done.prev_ref, bf16[136,512]{1,0:T(8,128)(2,1)S(1)} %shard_map.110.own_ref, ...), custom_call_target="tpu_custom_call" | custom-call | flops 100663296 | bytes 1499136 | tf_op jit(solution)/shard_map/pallas_call | solution.py:44
  25.2 0.0 collective-permute-done.11.other_ref
  25.2 0.5 shard_map.118
  25.7 2.5 %collective-permute-start.13 = (bf16[512,256]{1,0:T(8,128)(2,1)S(1)}, bf16[512,256]{1,0:T(8,128)(2,1)S(1)}, u32[]{:S(2)}, u32[]{:S(2)}) collective-permute-start(bf16[512,256]{1,0:T(8,128)(2,1)S(1)} %get-tuple-element.54), channel_id=1, source_target_pairs={{0,8},{8,0},{16,24},{24,16},{1,9},{9,1},{17,25},{25,17},{2,10},{10... | collective-permute-start | bytes 786440 | tf_op jit(solution)/shard_map/ppermute | solution.py:258
  28.1 0.0 collective-permute-done.2.rest_1_
  28.1 1.5 %collective-permute-start.14 = (bf16[512,256]{1,0:T(8,128)(2,1)S(1)}, bf16[512,256]{1,0:T(8,128)(2,1)S(1)}, u32[]{:S(2)}, u32[]{:S(2)}) collective-permute-start(bf16[512,256]{1,0:T(8,128)(2,1)S(1)} %get-tuple-element.55), channel_id=1, source_target_pairs={{0,16},{8,24},{16,0},{24,8},{1,17},{9,25},{17,1},{25,9},{2,18},{10... | collective-permute-start | bytes 786440 | tf_op jit(solution)/shard_map/ppermute | solution.py:258
  29.7 0.0 collective-permute-done.4.rest_3_
  29.7 0.0 collective-permute-start.15
  29.7 0.0 collective-permute-done.6.rest_5_
  29.7 2.2 %shard_map.114 = (bf16[384,256]{1,0:T(8,128)(2,1)S(1)}, f32[384,256]{1,0:T(8,128)S(1)}, bf16[384,768]{1,0:T(8,128)(2,1)S(1)}) custom-call(bf16[128,1024]{1,0:T(8,128)(2,1)S(1)} %get-tuple-element.33.q_ref, bf16[136,512]{1,0:T(8,128)(2,1)S(1)} %collective-permute-done.prev_ref, bf16[136,512]{1,0:T(8,128)(2,1)S(1)} %shard_map.110.own_ref, ...), custom_call_target="tpu_custom_call" | custom-call | flops 427819008 | bytes 5005312 | tf_op jit(solution)/shard_map/pallas_call | solution.py:44
  31.9 0.0 collective-permute-done.8.rest_1_.rest_7_
  31.9 1.0 %shard_map.115 = (bf16[128,512]{1,0:T(8,128)(2,1)S(1)}, bf16[128,512]{1,0:T(8,128)(2,1)S(1)}, bf16[128,512]{1,0:T(8,128)(2,1)S(1)}, bf16[384,256]{1,0:T(8,128)(2,1)S(1)}) custom-call(bf16[128,1024]{1,0:T(8,128)(2,1)S(1)} %get-tuple-element.33.q_ref, bf16[136,512]{1,0:T(8,128)(2,1)S(1)} %collective-permute-done.prev_ref, ...), custom_call_target="tpu_custom_call" | custom-call | flops 142606336 | bytes 3956736 | tf_op jit(solution)/shard_map/pallas_call | solution.py:44
  32.9 2.9 %collective-permute-start.9 = (bf16[128,512]{1,0:T(8,128)(2,1)S(1)}, bf16[128,512]{1,0:T(8,128)(2,1)S(1)}, u32[]{:S(2)}, u32[]{:S(2)}) collective-permute-start(bf16[128,512]{1,0:T(8,128)(2,1)S(1)} %get-tuple-element.49), channel_id=1, source_target_pairs={{0,24},{8,0},{16,8},{24,16},{1,25},{9,1},{17,9},{25,17},{2,26},{10... | collective-permute-start | bytes 393224 | tf_op jit(solution)/shard_map/ppermute | solution.py:263
  35.9 0.0 collective-permute-start.10
  35.9 0.0 collective-permute-done.13.refs_1_
  35.9 6.2 %collective-permute-done.14.refs_2_ = bf16[512,256]{1,0:T(8,128)(2,1)S(1)} collective-permute-done((bf16[512,256]{1,0:T(8,128)(2,1)S(1)}, bf16[512,256]{1,0:T(8,128)(2,1)S(1)}, u32[]{:S(2)}, u32[]{:S(2)}) %collective-permute-start.14) | collective-permute-done | bytes 262176 | tf_op jit(solution)/shard_map/ppermute | solution.py:258
  42.1 0.0 collective-permute-done.15.refs_3_
  42.1 0.1 shard_map.119
  42.3 1.2 %collective-permute-start.16 = (bf16[128,256]{1,0:T(8,128)(2,1)S(1)}, bf16[128,256]{1,0:T(8,128)(2,1)S(1)}, u32[]{:S(2)}, u32[]{:S(2)}) collective-permute-start(bf16[128,256]{1,0:T(8,128)(2,1)S(1)} %get-tuple-element.58), channel_id=1, source_target_pairs={{0,2},{1,3},{2,0},{3,1},{4,6},{5,7},{6,4},{7,5},{8,10},{9,11},{10,... | collective-permute-start | bytes 196616 | tf_op jit(solution)/shard_map/ppermute | solution.py:258
  43.4 3.1 %collective-permute-start.17 = (bf16[128,256]{1,0:T(8,128)(2,1)S(1)}, bf16[128,256]{1,0:T(8,128)(2,1)S(1)}, u32[]{:S(2)}, u32[]{:S(2)}) collective-permute-start(bf16[128,256]{1,0:T(8,128)(2,1)S(1)} %get-tuple-element.59), channel_id=1, source_target_pairs={{0,4},{1,5},{2,6},{3,7},{4,0},{5,1},{6,2},{7,3},{8,12},{9,13},{10,... | collective-permute-start | bytes 196616 | tf_op jit(solution)/shard_map/ppermute | solution.py:258
  46.5 0.5 collective-permute-start.18
  47.1 0.2 collective-permute-done.16.refs_1_
  47.3 3.9 %collective-permute-done.17.refs_2_ = bf16[128,256]{1,0:T(8,128)(2,1)S(1)} collective-permute-done((bf16[128,256]{1,0:T(8,128)(2,1)S(1)}, bf16[128,256]{1,0:T(8,128)(2,1)S(1)}, u32[]{:S(2)}, u32[]{:S(2)}) %collective-permute-start.17) | collective-permute-done | bytes 65568 | tf_op jit(solution)/shard_map/ppermute | solution.py:258
  51.1 1.5 %collective-permute-done.18.refs_3_ = bf16[128,256]{1,0:T(8,128)(2,1)S(1)} collective-permute-done((bf16[128,256]{1,0:T(8,128)(2,1)S(1)}, bf16[128,256]{1,0:T(8,128)(2,1)S(1)}, u32[]{:S(2)}, u32[]{:S(2)}) %collective-permute-start.18) | collective-permute-done | bytes 65568 | tf_op jit(solution)/shard_map/ppermute | solution.py:258
  52.6 0.7 %shard_map.120 = f32[128,256]{1,0:T(8,128)} custom-call(bf16[128,256]{1,0:T(8,128)(2,1)S(1)} %get-tuple-element.57.refs_0_, bf16[128,256]{1,0:T(8,128)(2,1)S(1)} %collective-permute-done.16.refs_1_, bf16[128,256]{1,0:T(8,128)(2,1)S(1)} %collective-permute-done.17.refs_2_, bf16[128,256]{1,0:T(8,128)(2,1)S(1)} %collective-permute-done.18.refs_3_), custom_call_target="tpu_custom_call" | custom-call | flops 1048576 | bytes 393216 | tf_op jit(solution)/shard_map/pallas_call | solution.py:44
  53.3 1.3 %shard_map.116 = (bf16[128,1024]{1,0:T(8,128)(2,1)}, bf16[128,1024]{1,0:T(8,128)(2,1)}) custom-call(bf16[136,512]{1,0:T(8,128)(2,1)S(1)} %collective-permute-done.prev_ref, bf16[136,512]{1,0:T(8,128)(2,1)S(1)} %shard_map.110.own_ref, bf16[136,512]{1,0:T(8,128)(2,1)S(1)} %collective-permute-done.1.next_ref, bf16[384,768]{1,0:T(8,128)(2,1)S(1)} %get-tuple-element.40.ds_ref, ...), custom_call_target="tpu_custom_call" | custom-call | flops 369098752 | bytes 4087808 | tf_op jit(solution)/shard_map/pallas_call | solution.py:44
  54.7 0.0 collective-permute-done.9.low_ref
  54.7 0.0 collective-permute-done.10.high_ref
  54.7 0.7 %shard_map.117 = (bf16[128,256]{1,0:T(8,128)(2,1)}, bf16[128,256]{1,0:T(8,128)(2,1)}) custom-call(bf16[128,512]{1,0:T(8,128)(2,1)S(1)} %get-tuple-element.48.own_ref, bf16[128,512]{1,0:T(8,128)(2,1)S(1)} %collective-permute-done.9.low_ref, bf16[128,512]{1,0:T(8,128)(2,1)S(1)} %collective-permute-done.10.high_ref), custom_call_target="tpu_custom_call" | custom-call | flops 1048576 | bytes 524288 | tf_op jit(solution)/shard_map/pallas_call | solution.py:44
Async XLA Ops:
  0.6 19.6 %copy-start = (bf16[128,1024]{1,0:T(8,128)(2,1)S(1)}, bf16[128,1024]{1,0:T(8,128)(2,1)}, u32[]{:S(2)}) copy-start(bf16[128,1024]{1,0:T(8,128)(2,1)} %rest_0_.3) | copy-start | bytes 786436
  0.6 16.4 %collective-permute-start.5 = (bf16[128,1024]{1,0:T(8,128)(2,1)}, bf16[128,1024]{1,0:T(8,128)(2,1)S(1)}, u32[]{:S(2)}, u32[]{:S(2)}) collective-permute-start(bf16[128,1024]{1,0:T(8,128)(2,1)} %rest_0_.3), channel_id=1, source_target_pairs={{0,4},{1,5},{2,6},{3,7},{4,0},{5,1},{6,2},{7,3},{8,12},{9,13},{10,... | collective-permute-start | bytes 786440 | tf_op jit(solution)/shard_map/ppermute | solution.py:258
  4.8 15.4 %collective-permute-start.3 = (bf16[128,1024]{1,0:T(8,128)(2,1)}, bf16[128,1024]{1,0:T(8,128)(2,1)S(1)}, u32[]{:S(2)}, u32[]{:S(2)}) collective-permute-start(bf16[128,1024]{1,0:T(8,128)(2,1)} %rest_0_.3), channel_id=1, source_target_pairs={{0,2},{1,3},{2,0},{3,1},{4,6},{5,7},{6,4},{7,5},{8,10},{9,11},{10,... | collective-permute-start | bytes 786440 | tf_op jit(solution)/shard_map/ppermute | solution.py:258
  7.3 12.9 %collective-permute-start = (bf16[136,512]{1,0:T(8,128)(2,1)S(1)}, bf16[136,512]{1,0:T(8,128)(2,1)S(1)}, u32[]{:S(2)}, u32[]{:S(2)}) collective-permute-start(bf16[136,512]{1,0:T(8,128)(2,1)S(1)} %shard_map.110.own_ref), channel_id=1, source_target_pairs={{0,8},{8,16},{16,24},{24,0},{1,9},{9,17},{17,25},{25,1},{2,10},{10... | collective-permute-start | bytes 417800 | tf_op jit(solution)/shard_map/ppermute | solution.py:263
  8.8 15.1 %collective-permute-start.12 = (bf16[128,1024]{1,0:T(8,128)(2,1)}, bf16[128,1024]{1,0:T(8,128)(2,1)S(1)}, u32[]{:S(2)}, u32[]{:S(2)}) collective-permute-start(bf16[128,1024]{1,0:T(8,128)(2,1)} %bitcast.11), channel_id=1, source_target_pairs={{0,1},{1,0},{2,3},{3,2},{4,5},{5,4},{6,7},{7,6},{8,9},{9,8},{10,11... | collective-permute-start | bytes 786440 | tf_op jit(solution)/shard_map/ppermute | solution.py:258
  17.0 7.4 %collective-permute-start.7 = (bf16[128,1024]{1,0:T(8,128)(2,1)S(1)}, bf16[128,1024]{1,0:T(8,128)(2,1)S(1)}, u32[]{:S(2)}, u32[]{:S(2)}) collective-permute-start(bf16[128,1024]{1,0:T(8,128)(2,1)S(1)} %collective-permute-done.5.rest_4_), channel_id=1, source_target_pairs={{0,2},{1,3},{2,0},{3,1},{4,6},{5,7},{6,4},{7,5},{8,10},{9,11},{10,... | collective-permute-start | bytes 786440 | tf_op jit(solution)/shard_map/ppermute | solution.py:258
  17.7 5.3 %collective-permute-start.1 = (bf16[136,512]{1,0:T(8,128)(2,1)S(1)}, bf16[136,512]{1,0:T(8,128)(2,1)S(1)}, u32[]{:S(2)}, u32[]{:S(2)}) collective-permute-start(bf16[136,512]{1,0:T(8,128)(2,1)S(1)} %shard_map.110.own_ref), channel_id=1, source_target_pairs={{0,24},{8,0},{16,8},{24,16},{1,25},{9,1},{17,9},{25,17},{2,26},{10... | collective-permute-start | bytes 417800 | tf_op jit(solution)/shard_map/ppermute | solution.py:263
  20.2 8.0 %collective-permute-start.2 = (bf16[128,1024]{1,0:T(8,128)(2,1)S(1)}, bf16[128,1024]{1,0:T(8,128)(2,1)S(1)}, u32[]{:S(2)}, u32[]{:S(2)}) collective-permute-start(bf16[128,1024]{1,0:T(8,128)(2,1)S(1)} %copy-done), channel_id=1, source_target_pairs={{0,1},{1,0},{2,3},{3,2},{4,5},{5,4},{6,7},{7,6},{8,9},{9,8},{10,11... | collective-permute-start | bytes 786440 | tf_op jit(solution)/shard_map/ppermute | solution.py:258
  20.2 9.5 %collective-permute-start.4 = (bf16[128,1024]{1,0:T(8,128)(2,1)S(1)}, bf16[128,1024]{1,0:T(8,128)(2,1)S(1)}, u32[]{:S(2)}, u32[]{:S(2)}) collective-permute-start(bf16[128,1024]{1,0:T(8,128)(2,1)S(1)} %collective-permute-done.3.rest_2_), channel_id=1, source_target_pairs={{0,1},{1,0},{2,3},{3,2},{4,5},{5,4},{6,7},{7,6},{8,9},{9,8},{10,11... | collective-permute-start | bytes 786440 | tf_op jit(solution)/shard_map/ppermute | solution.py:258
  23.8 1.4 %collective-permute-start.11 = (bf16[512,128]{1,0:T(8,128)(2,1)S(1)}, bf16[512,128]{1,0:T(8,128)(2,1)S(1)}, u32[]{:S(2)}, u32[]{:S(2)}) collective-permute-start(bf16[512,128]{1,0:T(8,128)(2,1)S(1)} %get-tuple-element.45.t1), channel_id=1, source_target_pairs={{0,1},{1,0},{2,3},{3,2},{4,5},{5,4},{6,7},{7,6},{8,9},{9,8},{10,11... | collective-permute-start | bytes 393224 | tf_op jit(solution)/shard_map/ppermute | solution.py:258
  23.9 5.8 %collective-permute-start.6 = (bf16[128,1024]{1,0:T(8,128)(2,1)S(1)}, bf16[128,1024]{1,0:T(8,128)(2,1)S(1)}, u32[]{:S(2)}, u32[]{:S(2)}) collective-permute-start(bf16[128,1024]{1,0:T(8,128)(2,1)S(1)} %collective-permute-done.5.rest_4_), channel_id=1, source_target_pairs={{0,1},{1,0},{2,3},{3,2},{4,5},{5,4},{6,7},{7,6},{8,9},{9,8},{10,11... | collective-permute-start | bytes 786440 | tf_op jit(solution)/shard_map/ppermute | solution.py:258
  24.4 7.5 %collective-permute-start.8 = (bf16[128,1024]{1,0:T(8,128)(2,1)S(1)}, bf16[128,1024]{1,0:T(8,128)(2,1)S(1)}, u32[]{:S(2)}, u32[]{:S(2)}) collective-permute-start(bf16[128,1024]{1,0:T(8,128)(2,1)S(1)} %collective-permute-done.7.rest_0_.rest_6_), channel_id=1, source_target_pairs={{0,1},{1,0},{2,3},{3,2},{4,5},{5,4},{6,7},{7,6},{8,9},{9,8},{10,11... | collective-permute-start | bytes 786440 | tf_op jit(solution)/shard_map/ppermute | solution.py:258
  25.7 10.2 %collective-permute-start.13 = (bf16[512,256]{1,0:T(8,128)(2,1)S(1)}, bf16[512,256]{1,0:T(8,128)(2,1)S(1)}, u32[]{:S(2)}, u32[]{:S(2)}) collective-permute-start(bf16[512,256]{1,0:T(8,128)(2,1)S(1)} %get-tuple-element.54), channel_id=1, source_target_pairs={{0,8},{8,0},{16,24},{24,16},{1,9},{9,1},{17,25},{25,17},{2,10},{10... | collective-permute-start | bytes 786440 | tf_op jit(solution)/shard_map/ppermute | solution.py:258
  28.1 14.0 %collective-permute-start.14 = (bf16[512,256]{1,0:T(8,128)(2,1)S(1)}, bf16[512,256]{1,0:T(8,128)(2,1)S(1)}, u32[]{:S(2)}, u32[]{:S(2)}) collective-permute-start(bf16[512,256]{1,0:T(8,128)(2,1)S(1)} %get-tuple-element.55), channel_id=1, source_target_pairs={{0,16},{8,24},{16,0},{24,8},{1,17},{9,25},{17,1},{25,9},{2,18},{10... | collective-permute-start | bytes 786440 | tf_op jit(solution)/shard_map/ppermute | solution.py:258
  29.7 12.5 %collective-permute-start.15 = (bf16[512,256]{1,0:T(8,128)(2,1)S(1)}, bf16[512,256]{1,0:T(8,128)(2,1)S(1)}, u32[]{:S(2)}, u32[]{:S(2)}) collective-permute-start(bf16[512,256]{1,0:T(8,128)(2,1)S(1)} %get-tuple-element.56), channel_id=1, source_target_pairs={{0,24},{8,16},{16,8},{24,0},{1,25},{9,17},{17,9},{25,1},{2,26},{10... | collective-permute-start | bytes 786440 | tf_op jit(solution)/shard_map/ppermute | solution.py:258
  32.9 21.7 %collective-permute-start.9 = (bf16[128,512]{1,0:T(8,128)(2,1)S(1)}, bf16[128,512]{1,0:T(8,128)(2,1)S(1)}, u32[]{:S(2)}, u32[]{:S(2)}) collective-permute-start(bf16[128,512]{1,0:T(8,128)(2,1)S(1)} %get-tuple-element.49), channel_id=1, source_target_pairs={{0,24},{8,0},{16,8},{24,16},{1,25},{9,1},{17,9},{25,17},{2,26},{10... | collective-permute-start | bytes 393224 | tf_op jit(solution)/shard_map/ppermute | solution.py:263
  35.9 18.8 %collective-permute-start.10 = (bf16[128,512]{1,0:T(8,128)(2,1)S(1)}, bf16[128,512]{1,0:T(8,128)(2,1)S(1)}, u32[]{:S(2)}, u32[]{:S(2)}) collective-permute-start(bf16[128,512]{1,0:T(8,128)(2,1)S(1)} %get-tuple-element.50), channel_id=1, source_target_pairs={{0,8},{8,16},{16,24},{24,0},{1,9},{9,17},{17,25},{25,1},{2,10},{10... | collective-permute-start | bytes 393224 | tf_op jit(solution)/shard_map/ppermute | solution.py:263
  42.3 5.0 %collective-permute-start.16 = (bf16[128,256]{1,0:T(8,128)(2,1)S(1)}, bf16[128,256]{1,0:T(8,128)(2,1)S(1)}, u32[]{:S(2)}, u32[]{:S(2)}) collective-permute-start(bf16[128,256]{1,0:T(8,128)(2,1)S(1)} %get-tuple-element.58), channel_id=1, source_target_pairs={{0,2},{1,3},{2,0},{3,1},{4,6},{5,7},{6,4},{7,5},{8,10},{9,11},{10,... | collective-permute-start | bytes 196616 | tf_op jit(solution)/shard_map/ppermute | solution.py:258
  43.4 7.7 %collective-permute-start.17 = (bf16[128,256]{1,0:T(8,128)(2,1)S(1)}, bf16[128,256]{1,0:T(8,128)(2,1)S(1)}, u32[]{:S(2)}, u32[]{:S(2)}) collective-permute-start(bf16[128,256]{1,0:T(8,128)(2,1)S(1)} %get-tuple-element.59), channel_id=1, source_target_pairs={{0,4},{1,5},{2,6},{3,7},{4,0},{5,1},{6,2},{7,3},{8,12},{9,13},{10,... | collective-permute-start | bytes 196616 | tf_op jit(solution)/shard_map/ppermute | solution.py:258
  46.5 6.1 %collective-permute-start.18 = (bf16[128,256]{1,0:T(8,128)(2,1)S(1)}, bf16[128,256]{1,0:T(8,128)(2,1)S(1)}, u32[]{:S(2)}, u32[]{:S(2)}) collective-permute-start(bf16[128,256]{1,0:T(8,128)(2,1)S(1)} %get-tuple-element.60), channel_id=1, source_target_pairs={{0,6},{1,7},{2,4},{3,5},{4,2},{5,3},{6,0},{7,1},{8,14},{9,15},{10,... | collective-permute-start | bytes 196616 | tf_op jit(solution)/shard_map/ppermute | solution.py:258
